TPU v7x, 512 devices: a whole 4x4x16 slice. The times are simulated.
512 devices in a mesh: dp: 16 (over x, y), expert: 32 (over z, core).
Axes of the slice: x: 4, y: 4, z: 16, core: 2. Of those that a mesh axis runs over, the one named last changes fastest.
Arguments:
- tokens: bfloat16 [16384, 3584], P('expert', 'dp'), may hold values from -6 to 6
- grad_out: bfloat16 [16384, 3584], P('expert', 'dp'), may hold values from -1.796875 to 1.796875
- expert_ids: int32 [16384, 8], P('expert'), may hold values from 0 to 255, as said below
- gates: float32 [16384, 8], P('expert'), may hold values from 0.25 to 2.5
- w_gate: bfloat16 [32, 3584, 1024], P('expert', 'dp'), may hold values from -0.09375 to 0.09375
- w_up: bfloat16 [32, 3584, 1024], P('expert', 'dp'), may hold values from -0.09375 to 0.09375
- w_down: bfloat16 [32, 1024, 3584], P('expert', None, 'dp'), may hold values from -0.1875 to 0.1875
Outputs:
- mixed: bfloat16 [16384, 3584], P('expert', 'dp')
- grad_tokens: bfloat16 [16384, 3584], P('expert', 'dp')
- grad_gate: bfloat16 [32, 3584, 1024], P('expert', 'dp')
- grad_up: bfloat16 [32, 3584, 1024], P('expert', 'dp')
- grad_down: bfloat16 [32, 1024, 3584], P('expert', None, 'dp')
Inputs may be any that keep to these rules, and one draw needn't show every extreme that they name: `expert_ids`: each row names 8 different experts, at most one of them below 32. Within each aligned block of 512 rows no expert below 32 is named by more than 32 rows, and one such expert, the same in every block, is named by exactly 32 rows of every block.
All inputs are finite; a program needn't handle non-finite values.
Results may differ from a plain program's by a relative error of at most 0.029.
Values may be sent and summed in bfloat16 or wider, within the bound.
A program may use at most 64 MiB of HBM per device.

v0:
```python
import jax
import jax.numpy as jnp
from jax import lax
from jax.sharding import PartitionSpec as P


def swish_gate(value):
    return value * jax.nn.sigmoid(value)


def swish_slope(value):
    logistic = jax.nn.sigmoid(value)
    return logistic * (1.0 + value * (1.0 - logistic))


def contract_rows(left, right):
    return lax.dot_general(
        left, right, (((0,), (0,)), ((), ())), preferred_element_type=jnp.float32
    )


def contract_cols(left, right):
    return lax.dot_general(
        left, right, (((1,), (1,)), ((), ())), preferred_element_type=jnp.float32
    )


def body(tokens, grad_out, expert_ids, gates, w_gate, w_up, w_down):
    experts = lax.axis_size("expert")
    tok_rows, features = tokens.shape
    capacity = tok_rows // 16
    slot_count = experts * capacity
    in_window = expert_ids < experts
    routed = jnp.any(in_window, axis=1)
    chosen = jnp.sum(jnp.where(in_window, expert_ids, 0), axis=1)
    weight_tok = jnp.sum(jnp.where(in_window, gates, jnp.zeros_like(gates)), axis=1)
    one_hot = (
        (chosen[:, None] == jnp.arange(experts, dtype=jnp.int32)[None, :]) & routed[:, None]
    ).astype(jnp.int32)
    position = jnp.sum((jnp.cumsum(one_hot, axis=0) - one_hot) * one_hot, axis=1)
    slot_index = jnp.where(routed, chosen * capacity + position, slot_count)
    source_row = jnp.full((slot_count,), tok_rows, jnp.int32)
    source_row = source_row.at[slot_index].set(jnp.arange(tok_rows, dtype=jnp.int32), mode="drop")
    scaled = (weight_tok[:, None] * grad_out.astype(jnp.float32)).astype(jnp.bfloat16)
    send_tokens = jnp.take(tokens, source_row, axis=0, mode="fill", fill_value=0).reshape(
        experts, capacity, features
    )
    send_grads = jnp.take(scaled, source_row, axis=0, mode="fill", fill_value=0).reshape(
        experts, capacity, features
    )
    arrived_tokens, arrived_grads = (
        lax.all_to_all(send_tokens, "expert", split_axis=0, concat_axis=0, tiled=True),
        lax.all_to_all(send_grads, "expert", split_axis=0, concat_axis=0, tiled=True),
    )
    expert_rows = arrived_tokens.reshape(slot_count, features)
    grad_rows_in = arrived_grads.reshape(slot_count, features)
    gate_mat = w_gate[0]
    up_mat = w_up[0]
    down_mat = w_down[0]
    part_gate = jnp.dot(expert_rows, gate_mat, preferred_element_type=jnp.float32)
    part_up = jnp.dot(expert_rows, up_mat, preferred_element_type=jnp.float32)
    gate_pre, up_pre = (
        lax.psum(part_gate.astype(jnp.bfloat16), "dp").astype(jnp.float32),
        lax.psum(part_up.astype(jnp.bfloat16), "dp").astype(jnp.float32),
    )
    full_act = (swish_gate(gate_pre) * up_pre).astype(jnp.bfloat16)
    expert_out = jnp.dot(full_act, down_mat, preferred_element_type=jnp.float32).astype(
        jnp.bfloat16
    )
    out_blocks = expert_out.reshape(experts, capacity, features)
    back_out = lax.all_to_all(out_blocks, "expert", split_axis=0, concat_axis=0, tiled=True)
    grad_down = contract_rows(full_act, grad_rows_in).astype(jnp.bfloat16)
    part_act = contract_cols(grad_rows_in, down_mat)
    grad_act = lax.psum(part_act.astype(jnp.bfloat16), "dp").astype(jnp.float32)
    grad_gate_pre = (grad_act * up_pre * swish_slope(gate_pre)).astype(jnp.bfloat16)
    grad_up_pre = (grad_act * swish_gate(gate_pre)).astype(jnp.bfloat16)
    grad_gate = contract_rows(expert_rows, grad_gate_pre).astype(jnp.bfloat16)
    grad_up = contract_rows(expert_rows, grad_up_pre).astype(jnp.bfloat16)
    row_grad = (contract_cols(grad_gate_pre, gate_mat) + contract_cols(grad_up_pre, up_mat)).astype(
        jnp.bfloat16
    )
    grad_blocks = row_grad.reshape(experts, capacity, features)
    back_grad = lax.all_to_all(grad_blocks, "expert", split_axis=0, concat_axis=0, tiled=True)
    token_out = jnp.take(
        back_out.reshape(slot_count, features), slot_index, axis=0, mode="fill", fill_value=0
    )
    mixed = (weight_tok[:, None] * token_out.astype(jnp.float32)).astype(jnp.bfloat16)
    grad_tokens = jnp.take(
        back_grad.reshape(slot_count, features), slot_index, axis=0, mode="fill", fill_value=0
    )
    return (mixed, grad_tokens, grad_gate[None], grad_up[None], grad_down[None])


def solution(mesh):
    placed = (
        P("expert", "dp"),
        P("expert", "dp"),
        P("expert", None),
        P("expert", None),
        P("expert", "dp", None),
        P("expert", "dp", None),
        P("expert", None, "dp"),
    )
    return jax.shard_map(
        body,
        mesh=mesh,
        in_specs=placed,
        out_specs=(
            P("expert", "dp"),
            P("expert", "dp"),
            P("expert", "dp", None),
            P("expert", "dp", None),
            P("expert", None, "dp"),
        ),
        check_vma=False,
    )
```

profile of v0, /device:TPU:1, one launch (start us, length us, event | category | flops | bytes accessed | tf_op | source)
XLA Modules:
  0.0 363.5 jit_solution(16019415011018475140)
XLA Ops:
  7.2 0.0 copy-start
  7.2 0.8 select_reduce_fusion
  8.0 0.7 fusion.29
  8.7 1.2 reduce-window.6
  9.9 0.2 slice_reduce_fusion
  10.2 0.1 fusion.22
  10.3 2.4 scatter_custom_fusion
  12.8 0.8 select_reduce_fusion.1
  13.5 1.1 copy.21
  14.6 1.1 copy.19
  15.7 0.1 multiply_convert_fusion
  15.8 3.9 %gather_fusion.2 = bf16[1024,224]{1,0:T(8,128)(2,1)S(1)} fusion(bf16[512,224]{1,0:T(8,128)(2,1)S(1)} %multiply_convert_fusion, s32[1024]{0:T(1024)S(1)} %fusion.26), kind=kCustom, calls=%fused_computation.2.clone | custom fusion | bytes 921600 | tf_op jit(solution)/shard_map/jit(_take)/gather | solution.py:48
  19.8 3.9 %gather_fusion = bf16[1024,224]{1,0:T(8,128)(2,1)S(1)} fusion(bf16[512,224]{1,0:T(8,128)(2,1)S(1)} %copy.19, s32[1024]{0:T(1024)S(1)} %fusion.26), kind=kCustom, calls=%fused_computation.clone | custom fusion | bytes 921600 | tf_op jit(solution)/shard_map/jit(_take)/gather | solution.py:45
  23.7 0.0 copy-start.7
  23.7 1.0 broadcast_select_fusion
  24.7 50.0 %all_to_all.20 = bf16[32,32,224]{2,1,0:T(8,128)(2,1)S(1)} all-to-all(bf16[32,32,224]{2,1,0:T(8,128)(2,1)S(1)} %bitcast.73), channel_id=1, replica_groups=mesh['dp'=16,'expert'=32] {'expert'}, dimensions={0} | all-to-all | bytes 917504 | tf_op jit(solution)/shard_map/all_to_all | solution.py:52
  74.8 4.0 %all-to-all-start.2 = ((bf16[32,32,224]{2,1,0:T(8,128)(2,1)}), bf16[32,32,224]{2,1,0:T(8,128)(2,1)S(1)}, u32[]{:S(2)}, u32[]{:S(2)}) async-start(bf16[32,32,224]{2,1,0:T(8,128)(2,1)} %bitcast.12), calls=%async_computation.2 | async-start | bytes 1048576 | tf_op jit(solution)/shard_map/all_to_all | solution.py:53
  78.8 0.0 all-reduce.3.cloned.1.call-start
  78.9 0.0 copy-done.7
  78.9 2.1 convolution_convert_fusion.1
  81.0 2.0 convolution_convert_fusion.2
  83.0 29.4 %all-to-all-done.2 = bf16[32,32,224]{2,1,0:T(8,128)(2,1)S(1)} async-done(((bf16[32,32,224]{2,1,0:T(8,128)(2,1)}), bf16[32,32,224]{2,1,0:T(8,128)(2,1)S(1)}, u32[]{:S(2)}, u32[]{:S(2)}) %all-to-all-start.2) | async-done | bytes 458784 | tf_op jit(solution)/shard_map/all_to_all | solution.py:53
  112.4 2.0 convolution_convert_fusion
  114.4 0.0 all-reduce.3.cloned.1.call-update
  114.4 0.0 copy-done.4
  114.4 144.9 %all-reduce.3.cloned.1.call-done = (bf16[1024,1024]{1,0:T(8,128)(2,1)}, bf16[1024,1024]{1,0:T(8,128)(2,1)}, bf16[1024,1024]{1,0:T(8,128)(2,1)}) async-done(((bf16[1024,1024]{1,0:T(8,128)(2,1)}, bf16[1024,1024]{1,0:T(8,128)(2,1)}, bf16[1024,1024]{1,0:T(8,128)(2,1)}), (bf16[1024,1024]{1,0:T(8,128)(2,1)}, bf16[1024,1024]{1,0:T(8,128)(2,1)}, bf16[1024,1024]{1,0:T(8,128)(2,1)})) %all-reduce.3.cloned.1.call-update) | async-done | bytes 6291472 | tf_op jit(solution)/shard_map/psum | solution.py:64
  259.4 5.6 %fusion.3 = (bf16[1024,1024]{1,0:T(8,128)(2,1)S(1)}, bf16[1024,1024]{1,0:T(8,128)(2,1)S(1)}, bf16[1024,1024]{1,0:T(8,128)(2,1)}) fusion(bf16[1024,1024]{1,0:T(8,128)(2,1)} %get-tuple-element.19, bf16[1024,1024]{1,0:T(8,128)(2,1)} %get-tuple-element.18, bf16[1024,1024]{1,0:T(8,128)(2,1)} %get-tuple-element.17), kind=kLoop, calls=%fused_computation.14 | loop fusion | flops 18874368 | bytes 12582912 | tf_op jit(solution)/shard_map/convert_element_type | solution.py:76
  265.0 0.8 fusion.17
  265.8 0.5 copy-done.1
  266.3 0.8 fusion.9
  267.1 1.0 copy.22
  268.1 13.0 %all-to-all-start.3 = ((bf16[32,32,224]{2,1,0:T(8,128)(2,1)}), bf16[32,32,224]{2,1,0:T(8,128)(2,1)S(1)}, u32[]{:S(2)}, u32[]{:S(2)}) async-start(bf16[32,32,224]{2,1,0:T(8,128)(2,1)} %bitcast.70), calls=%async_computation.3 | async-start | bytes 1048576 | tf_op jit(solution)/shard_map/all_to_all | solution.py:83
  281.1 2.5 convolution_convert_fusion.6
  283.6 1.0 copy.20
  284.6 30.0 %all-to-all-done.3 = bf16[32,32,224]{2,1,0:T(8,128)(2,1)S(1)} async-done(((bf16[32,32,224]{2,1,0:T(8,128)(2,1)}), bf16[32,32,224]{2,1,0:T(8,128)(2,1)S(1)}, u32[]{:S(2)}, u32[]{:S(2)}) %all-to-all-start.3) | async-done | bytes 458784 | tf_op jit(solution)/shard_map/all_to_all | solution.py:83
  314.6 4.7 %all-to-all-start.1 = ((bf16[32,32,224]{2,1,0:T(8,128)(2,1)}), bf16[32,32,224]{2,1,0:T(8,128)(2,1)}, u32[]{:S(2)}, u32[]{:S(2)}) async-start(bf16[32,32,224]{2,1,0:T(8,128)(2,1)} %bitcast.69), calls=%async_computation.1 | async-start | bytes 1048576 | tf_op jit(solution)/shard_map/all_to_all | solution.py:71
  319.3 0.0 copy-start.3
  319.4 3.2 fusion.10
  322.6 1.4 fusion.11
  324.1 0.5 copy-done.6
  324.6 1.5 fusion.12
  326.0 1.9 gather_fusion.3
  328.0 0.1 broadcast_select_fusion.2
  328.1 0.8 copy.24
  328.9 24.0 %all-to-all-done.1 = bf16[32,32,224]{2,1,0:T(8,128)(2,1)} async-done(((bf16[32,32,224]{2,1,0:T(8,128)(2,1)}), bf16[32,32,224]{2,1,0:T(8,128)(2,1)}, u32[]{:S(2)}, u32[]{:S(2)}) %all-to-all-start.1) | async-done | bytes 458784 | tf_op jit(solution)/shard_map/all_to_all | solution.py:71
  352.9 2.7 gather_fusion.1
  355.6 0.2 multiply_convert_fusion.1
  355.8 0.8 copy.23
  (21 shorter events, 0.1 us)
Async XLA Ops:
  7.2 73.8 %copy-start = (bf16[1,224,1024]{2,1,0:T(8,128)(2,1)S(1)}, bf16[1,224,1024]{2,1,0:T(8,128)(2,1)}, u32[]{:S(2)}) copy-start(bf16[1,224,1024]{2,1,0:T(8,128)(2,1)} %param.15) | copy-start | bytes 1376260
  23.7 55.2 %copy-start.7 = (bf16[1,224,1024]{2,1,0:T(8,128)(2,1)S(1)}, bf16[1,224,1024]{2,1,0:T(8,128)(2,1)}, u32[]{:S(2)}) copy-start(bf16[1,224,1024]{2,1,0:T(8,128)(2,1)} %param.16) | copy-start | bytes 1376260
  74.8 8.2 %copy-start.2 = (bf16[32,32,224]{2,1,0:T(8,128)(2,1)}, bf16[32,32,224]{2,1,0:T(8,128)(2,1)S(1)}, u32[]{:S(2)}) copy-start(bf16[32,32,224]{2,1,0:T(8,128)(2,1)S(1)} %all_to_all.20) | copy-start | bytes 1376260
  74.8 37.6 %all-to-all-start.2 = ((bf16[32,32,224]{2,1,0:T(8,128)(2,1)}), bf16[32,32,224]{2,1,0:T(8,128)(2,1)S(1)}, u32[]{:S(2)}, u32[]{:S(2)}) async-start(bf16[32,32,224]{2,1,0:T(8,128)(2,1)} %bitcast.12), calls=%async_computation.2 | async-start | bytes 1048576 | tf_op jit(solution)/shard_map/all_to_all | solution.py:53
  78.8 180.5 %all-reduce.3.cloned.1.call-start = ((), (), s32[]{:S(2)}) async-start(), calls=%async_computation.4 | async-start | bytes 12582912 | tf_op jit(solution)/shard_map/psum | solution.py:64
  81.0 31.4 %copy-start.8 = (bf16[1,1024,224]{1,2,0:T(8,128)(2,1)S(1)}, bf16[1,1024,224]{1,2,0:T(8,128)(2,1)}, u32[]{:S(2)}) copy-start(bf16[1,1024,224]{1,2,0:T(8,128)(2,1)} %param.17) | copy-start | bytes 1376260
  112.4 2.0 copy-start.4
  265.0 1.3 copy-start.1
  268.1 46.5 %all-to-all-start.3 = ((bf16[32,32,224]{2,1,0:T(8,128)(2,1)}), bf16[32,32,224]{2,1,0:T(8,128)(2,1)S(1)}, u32[]{:S(2)}, u32[]{:S(2)}) async-start(bf16[32,32,224]{2,1,0:T(8,128)(2,1)} %bitcast.70), calls=%async_computation.3 | async-start | bytes 1048576 | tf_op jit(solution)/shard_map/all_to_all | solution.py:83
  314.6 38.3 %all-to-all-start.1 = ((bf16[32,32,224]{2,1,0:T(8,128)(2,1)}), bf16[32,32,224]{2,1,0:T(8,128)(2,1)}, u32[]{:S(2)}, u32[]{:S(2)}) async-start(bf16[32,32,224]{2,1,0:T(8,128)(2,1)} %bitcast.69), calls=%async_computation.1 | async-start | bytes 1048576 | tf_op jit(solution)/shard_map/all_to_all | solution.py:71
  319.3 3.3 copy-start.3
  322.6 1.4 copy-start.5
  322.6 1.9 copy-start.6
Sparse Core Ops, SparseCore 0:
  114.5 144.7 all-reduce.2
where the time goes:
time: 364 us; the launch traced here: 363 us
  waiting for transfers between devices  228 us (63%)
  blocking collectives  50 us (14%)
  local copies, waits for them, and re-layouts  22 us (6%)
  starting transfers between devices  21.8 us (6%)
  matrix products  16.2 us (4%)
  between operations  14.3 us (4%)
  other arithmetic  10.7 us (3%)
    psum x1, waiting for transfers between devices, body(): lax.psum(part_up.astype(jnp.bfloat16), 'dp').astype(jnp.float32)  145 us
    all_to_all x1, blocking collectives, body(): lax.all_to_all(send_tokens, 'expert', split_axis=0, concat_axis=0, tiled=...  50 us
    all_to_all x1, waiting for transfers between devices, body(): lax.all_to_all(grad_blocks, 'expert', split_axis=0, concat_axis=0, tiled=...  30 us
    all_to_all x1, waiting for transfers between devices, body(): lax.all_to_all(send_grads, 'expert', split_axis=0, concat_axis=0, tiled=T...  29.4 us
    all_to_all x1, waiting for transfers between devices, body(): lax.all_to_all(out_blocks, 'expert', split_axis=0, concat_axis=0, tiled=T...  24 us
    all_to_all x1, starting transfers between devices, body(): lax.all_to_all(grad_blocks, 'expert', split_axis=0, concat_axis=0, tiled=...  13 us
  transfers between devices with their start and end apart: 4, of which 4 were waited for; matrix products, arithmetic and copies ran while one was open for 5% of the time, Pallas kernels for 0%

commit v1 on v0

--- a/solution.py
+++ b/solution.py
@@ -61,7 +61,9 @@
     part_up = jnp.dot(expert_rows, up_mat, preferred_element_type=jnp.float32)
     gate_pre, up_pre = (
         lax.psum(part_gate.astype(jnp.bfloat16), "dp").astype(jnp.float32),
-        lax.psum(part_up.astype(jnp.bfloat16), "dp").astype(jnp.float32),
+        jnp.sum(lax.all_gather(part_up.astype(jnp.bfloat16), axis_name="dp"), axis=0).astype(
+            jnp.float32
+        ),
     )
     full_act = (swish_gate(gate_pre) * up_pre).astype(jnp.bfloat16)
     expert_out = jnp.dot(full_act, down_mat, preferred_element_type=jnp.float32).astype(

time: 364 us -> 523 us (1.44)
  waiting for transfers between devices: 228 us -> 374 us
  other arithmetic: 10.7 us -> 23.7 us
    all_gather x0 -> x1, waiting for transfers between devices: none -> 164 us  [body(): lax.all_gather(part_up.astype(jnp.bfloat16), axis_name='dp')]
    psum x1, waiting for transfers between devices: 145 us -> 124 us  [body(): lax.psum(part_gate.astype(jnp.bfloat16), 'dp').astype(jnp.float32)]
    reduce_sum x0 -> x1, other arithmetic: none -> 13 us  [body(): jnp.sum(lax.all_gather(part_up.astype(jnp.bfloat16), axis_name='dp'), axi...]
  transfers between devices with their start and end apart: 4 -> 5, of which waited for: 4 -> 5; matrix products, arithmetic and copies ran while one was open for 5% -> 6% of each run, Pallas kernels for 0% -> 0%
where the time goes in v1:
time: 523 us
  waiting for transfers between devices  374 us (72%)
  blocking collectives  50 us (10%)
  other arithmetic  23.7 us (5%)
  local copies, waits for them, and re-layouts  22.1 us (4%)
  starting transfers between devices  22.1 us (4%)
  matrix products  16.2 us (3%)
  between operations  14.3 us (3%)
    all_gather x1, waiting for transfers between devices, body(): lax.all_gather(part_up.astype(jnp.bfloat16), axis_name='dp')  164 us
    psum x1, waiting for transfers between devices, body(): lax.psum(part_gate.astype(jnp.bfloat16), 'dp').astype(jnp.float32)  124 us
    all_to_all x1, blocking collectives, body(): lax.all_to_all(send_tokens, 'expert', split_axis=0, concat_axis=0, tiled=...  50 us
    all_to_all x1, waiting for transfers between devices, body(): lax.all_to_all(send_grads, 'expert', split_axis=0, concat_axis=0, tiled=T...  31.5 us
    all_to_all x1, waiting for transfers between devices, body(): lax.all_to_all(grad_blocks, 'expert', split_axis=0, concat_axis=0, tiled=...  30 us
    all_to_all x1, waiting for transfers between devices, body(): lax.all_to_all(out_blocks, 'expert', split_axis=0, concat_axis=0, tiled=T...  24 us
    all_to_all x1, starting transfers between devices, body(): lax.all_to_all(grad_blocks, 'expert', split_axis=0, concat_axis=0, tiled=...  13.2 us
    reduce_sum x1, other arithmetic, body(): jnp.sum(lax.all_gather(part_up.astype(jnp.bfloat16), axis_name='dp'), axi...  13 us
  transfers between devices with their start and end apart: 5, of which 5 were waited for; matrix products, arithmetic and copies ran while one was open for 6% of the time, Pallas kernels for 0%

profile of v1, /device:TPU:1, one launch (start us, length us, event | category | flops | bytes accessed | tf_op | source)
XLA Modules:
  0.0 522.5 jit_solution(9994099560127778587)
XLA Ops:
  7.2 0.0 copy-start
  7.2 0.0 all-gather.3.cloned.1.call-start
  7.2 0.8 fusion.29
  8.0 0.7 select_reduce_fusion
  8.8 1.2 reduce-window.6
  9.9 0.2 slice_reduce_fusion
  10.2 0.1 fusion.22
  10.3 2.4 scatter_custom_fusion
  12.8 0.8 select_reduce_fusion.1
  13.6 1.1 copy.19
  14.7 1.1 copy.21
  15.7 3.9 gather_fusion
  19.7 0.1 multiply_convert_fusion
  19.8 3.9 gather_fusion.2
  23.8 1.0 broadcast_select_fusion
  24.8 50.0 %all_to_all.20 = bf16[32,32,224]{2,1,0:T(8,128)(2,1)S(1)} all-to-all(bf16[32,32,224]{2,1,0:T(8,128)(2,1)S(1)} %bitcast.76), channel_id=1, replica_groups=mesh['dp'=16,'expert'=32] {'expert'}, dimensions={0} | all-to-all | bytes 917504 | tf_op jit(solution)/shard_map/all_to_all | solution.py:52
  74.9 2.0 convolution_convert_fusion.1
  76.9 0.0 all-gather.3.cloned.1.call-update
  76.9 4.2 all-to-all-start.2
  81.1 0.0 all-reduce.3.cloned.1.call-start
  81.2 2.0 convolution_convert_fusion.2
  83.2 31.5 %all-to-all-done.2 = bf16[32,32,224]{2,1,0:T(8,128)(2,1)S(1)} async-done(((bf16[32,32,224]{2,1,0:T(8,128)(2,1)}), bf16[32,32,224]{2,1,0:T(8,128)(2,1)S(1)}, u32[]{:S(2)}, u32[]{:S(2)}) %all-to-all-start.2) | async-done | bytes 458784 | tf_op jit(solution)/shard_map/all_to_all | solution.py:53
  114.6 2.1 convolution_convert_fusion
  116.7 0.0 all-reduce.3.cloned.1.call-update
  116.7 164.0 %all-gather.3.cloned.1.call-done = bf16[16384,1024]{1,0:T(8,128)(2,1)} async-done(((bf16[1024,1024]{1,0:T(8,128)(2,1)}), bf16[16384,1024]{1,0:T(8,128)(2,1)}) %all-gather.3.cloned.1.call-update) | async-done | bytes 33554448 | tf_op jit(solution)/shard_map/all_gather | solution.py:64
  280.8 13.0 %reduce_sum.42 = bf16[1024,1024]{1,0:T(8,128)(2,1)} reduce(bf16[16,1024,1024]{2,1,0:T(8,128)(2,1)} %bitcast.66, bf16[]{:T(256)} %constant.14.clone.1), dimensions={0}, to_apply=%region_8.10 | reduce | flops 15728640 | bytes 35651584 | tf_op jit(solution)/shard_map/reduce_sum | solution.py:64
  293.8 124.5 %all-reduce.3.cloned.1.call-done = (bf16[1024,1024]{1,0:T(8,128)(2,1)}, bf16[1024,1024]{1,0:T(8,128)(2,1)}) async-done(((bf16[1024,1024]{1,0:T(8,128)(2,1)}, bf16[1024,1024]{1,0:T(8,128)(2,1)}), (bf16[1024,1024]{1,0:T(8,128)(2,1)}, bf16[1024,1024]{1,0:T(8,128)(2,1)})) %all-reduce.3.cloned.1.call-update) | async-done | bytes 4194320 | tf_op jit(solution)/shard_map/psum | solution.py:63
  418.3 5.6 %fusion.3 = (bf16[1024,1024]{1,0:T(8,128)(2,1)S(1)}, bf16[1024,1024]{1,0:T(8,128)(2,1)S(1)}, bf16[1024,1024]{1,0:T(8,128)(2,1)}) fusion(bf16[1024,1024]{1,0:T(8,128)(2,1)} %get-tuple-element.18, bf16[1024,1024]{1,0:T(8,128)(2,1)} %get-tuple-element.17, bf16[1024,1024]{1,0:T(8,128)(2,1)} %reduce_sum.42), kind=kLoop, calls=%fused_computation.14 | loop fusion | flops 18874368 | bytes 12582912 | tf_op jit(solution)/shard_map/convert_element_type | solution.py:78
  423.8 0.8 fusion.17
  424.6 0.6 copy-done.1
  425.2 0.8 fusion.9
  426.0 1.0 copy.22
  427.0 13.2 %all-to-all-start.3 = ((bf16[32,32,224]{2,1,0:T(8,128)(2,1)}), bf16[32,32,224]{2,1,0:T(8,128)(2,1)S(1)}, u32[]{:S(2)}, u32[]{:S(2)}) async-start(bf16[32,32,224]{2,1,0:T(8,128)(2,1)} %bitcast.73), calls=%async_computation.3 | async-start | bytes 1048576 | tf_op jit(solution)/shard_map/all_to_all | solution.py:85
  440.2 2.5 convolution_convert_fusion.6
  442.6 1.0 copy.20
  443.7 30.0 %all-to-all-done.3 = bf16[32,32,224]{2,1,0:T(8,128)(2,1)S(1)} async-done(((bf16[32,32,224]{2,1,0:T(8,128)(2,1)}), bf16[32,32,224]{2,1,0:T(8,128)(2,1)S(1)}, u32[]{:S(2)}, u32[]{:S(2)}) %all-to-all-start.3) | async-done | bytes 458784 | tf_op jit(solution)/shard_map/all_to_all | solution.py:85
  473.7 4.7 all-to-all-start.1
  478.4 3.2 fusion.11
  481.7 1.4 fusion.10
  483.1 0.5 copy-done.6
  483.6 1.5 fusion.12
  485.1 1.9 gather_fusion.3
  487.0 0.1 broadcast_select_fusion.2
  487.2 0.8 copy.24
  488.0 24.0 %all-to-all-done.1 = bf16[32,32,224]{2,1,0:T(8,128)(2,1)} async-done(((bf16[32,32,224]{2,1,0:T(8,128)(2,1)}), bf16[32,32,224]{2,1,0:T(8,128)(2,1)}, u32[]{:S(2)}, u32[]{:S(2)}) %all-to-all-start.1) | async-done | bytes 458784 | tf_op jit(solution)/shard_map/all_to_all | solution.py:73
  512.0 2.7 gather_fusion.1
  514.7 0.2 multiply_convert_fusion.1
  514.9 0.8 copy.23
  (25 shorter events, 0.1 us)
Async XLA Ops:
  7.2 74.0 %copy-start = (bf16[1,224,1024]{2,1,0:T(8,128)(2,1)S(1)}, bf16[1,224,1024]{2,1,0:T(8,128)(2,1)}, u32[]{:S(2)}) copy-start(bf16[1,224,1024]{2,1,0:T(8,128)(2,1)} %param.15) | copy-start | bytes 1376260
  7.2 273.6 %all-gather.3.cloned.1.call-start = ((), (), s32[]{:S(2)}) async-start(), calls=%async_computation.4 | async-start | bytes 35651584 | tf_op jit(solution)/shard_map/all_gather | solution.py:64
  23.8 51.1 %copy-start.7 = (bf16[1,224,1024]{2,1,0:T(8,128)(2,1)S(1)}, bf16[1,224,1024]{2,1,0:T(8,128)(2,1)}, u32[]{:S(2)}) copy-start(bf16[1,224,1024]{2,1,0:T(8,128)(2,1)} %param.16) | copy-start | bytes 1376260
  74.9 6.3 %copy-start.2 = (bf16[32,32,224]{2,1,0:T(8,128)(2,1)}, bf16[32,32,224]{2,1,0:T(8,128)(2,1)S(1)}, u32[]{:S(2)}) copy-start(bf16[32,32,224]{2,1,0:T(8,128)(2,1)S(1)} %all_to_all.20) | copy-start | bytes 1376260
  76.9 37.7 %copy-start.8 = (bf16[1,1024,224]{1,2,0:T(8,128)(2,1)S(1)}, bf16[1,1024,224]{1,2,0:T(8,128)(2,1)}, u32[]{:S(2)}) copy-start(bf16[1,1024,224]{1,2,0:T(8,128)(2,1)} %param.17) | copy-start | bytes 1376260
  76.9 37.7 %all-to-all-start.2 = ((bf16[32,32,224]{2,1,0:T(8,128)(2,1)}), bf16[32,32,224]{2,1,0:T(8,128)(2,1)S(1)}, u32[]{:S(2)}, u32[]{:S(2)}) async-start(bf16[32,32,224]{2,1,0:T(8,128)(2,1)} %bitcast.13), calls=%async_computation.2 | async-start | bytes 1048576 | tf_op jit(solution)/shard_map/all_to_all | solution.py:53
  81.1 337.2 %all-reduce.3.cloned.1.call-start = ((), (), s32[]{:S(2)}) async-start(), calls=%async_computation.5 | async-start | bytes 8388608 | tf_op jit(solution)/shard_map/psum | solution.py:63
  114.6 2.1 copy-start.4
  423.8 1.4 copy-start.1
  427.0 46.7 %all-to-all-start.3 = ((bf16[32,32,224]{2,1,0:T(8,128)(2,1)}), bf16[32,32,224]{2,1,0:T(8,128)(2,1)S(1)}, u32[]{:S(2)}, u32[]{:S(2)}) async-start(bf16[32,32,224]{2,1,0:T(8,128)(2,1)} %bitcast.73), calls=%async_computation.3 | async-start | bytes 1048576 | tf_op jit(solution)/shard_map/all_to_all | solution.py:85
  473.7 38.3 %all-to-all-start.1 = ((bf16[32,32,224]{2,1,0:T(8,128)(2,1)}), bf16[32,32,224]{2,1,0:T(8,128)(2,1)}, u32[]{:S(2)}, u32[]{:S(2)}) async-start(bf16[32,32,224]{2,1,0:T(8,128)(2,1)} %bitcast.72), calls=%async_computation.1 | async-start | bytes 1048576 | tf_op jit(solution)/shard_map/all_to_all | solution.py:73
  478.4 3.3 copy-start.3
  481.7 1.4 copy-start.5
  481.7 1.9 copy-start.6
Sparse Core Ops, SparseCore 0:
  77.0 203.7 all-gather.2
  284.2 134.0 all-reduce.2
